TPU v7x, 256 devices: a whole 4x4x8 slice. The times are simulated.
256 devices in a mesh: dp: 8 (over y, core), expert: 32 (over x, z).
Axes of the slice: x: 4, y: 4, z: 8, core: 2. Of those that a mesh axis runs over, the one named last changes fastest.
Arguments:
- tokens: bfloat16 [8192, 3584], P('expert', 'dp'), may hold values from -6 to 6
- cotangent: bfloat16 [8192, 3584], P('expert', 'dp'), may hold values from -6 to 6
- slot_tokens: int32 [32, 32, 32], P('expert'), may hold values from 0 to 255
- slot_counts: int32 [32, 32], P('expert'), may hold values from 0 to 32, as said below
- slot_gates: float32 [32, 32, 32], P('expert'), may hold values from 0.1 to 1
- swap_pairs: int32 [16], replicated, may hold values from 0 to 1, as said below
- gate_weight: bfloat16 [32, 3584, 1024], P('expert', 'dp'), may hold values from -0.09375 to 0.09375
- up_weight: bfloat16 [32, 3584, 1024], P('expert', 'dp'), may hold values from -0.09375 to 0.09375
- down_weight: bfloat16 [32, 1024, 3584], P('expert', None, 'dp'), may hold values from -0.1875 to 0.1875
- first_moment: float32 [32, 1024, 3584], P('expert', None, 'dp'), may hold values from -6 to 6
- second_moment: float32 [32, 1024, 3584], P('expert', None, 'dp'), may hold values from 0.5 to 4
Outputs:
- mixed: bfloat16 [8192, 3584], P('expert', 'dp')
- token_grad: bfloat16 [8192, 3584], P('expert', 'dp')
- new_first_moment: float32 [32, 1024, 3584], P('expert', None, 'dp')
- new_second_moment: float32 [32, 1024, 3584], P('expert', None, 'dp')
- adam_step: bfloat16 [32, 1024, 3584], P('expert', None, 'dp')
Inputs may be any that keep to these rules, and one draw needn't show every extreme that they name: `slot_tokens`: slots at or past slot_counts hold arbitrary token numbers and carry nothing. `slot_counts`: every source fills all 32 slots of some expert, and one expert receives 32 live slots from every source. `swap_pairs`: at least one pair trades and at least one pair does not.
All inputs are finite; a program needn't handle non-finite values.
Results may differ from a plain program's by a relative error of at most 0.022.
Values may be sent and summed in bfloat16 or wider, within the bound.
No kernel may reach another device: no remote copies, remote signals or barrier semaphores. Data moves between devices by JAX's collectives and lax.ppermute only.
A program may use at most 128 MiB of HBM per device.

v0:
```python
import jax
import jax.numpy as jnp
from jax import lax
from jax.sharding import PartitionSpec as P

beta_first = 0.9
beta_second = 0.999
adam_eps = 1e-08


def partner(block, axis, bit):
    count = lax.axis_size(axis)
    route = []
    for low in range(count):
        high = low | 1 << bit
        if high != low and high < count:
            route += [(low, high), (high, low)]
    return lax.ppermute(block, axis, route)


def held_order(values, pair_flags):
    half_count = pair_flags.shape[0]
    blocks = values.reshape((2, half_count) + values.shape[1:])
    chosen = pair_flags.reshape((1, half_count) + (1,) * (values.ndim - 1)) > 0
    return jnp.where(chosen, blocks[::-1], blocks).reshape(values.shape)


def preact_grad(hidden_grad, gate_pre, up_pre):
    sigmoid_gate = jax.nn.sigmoid(gate_pre)
    first_half = hidden_grad * up_pre * sigmoid_gate * (1.0 + gate_pre * (1.0 - sigmoid_gate))
    second_half = hidden_grad * gate_pre * sigmoid_gate
    return jnp.concatenate([first_half, second_half], axis=1).astype(jnp.bfloat16)


def shards(
    tokens,
    cotangent,
    slot_tokens,
    slot_counts,
    slot_gates,
    swap_pairs,
    gate_weight,
    up_weight,
    down_weight,
    first_moment,
    second_moment,
):
    tok_count, model_cols = tokens.shape
    experts = slot_counts.shape[1]
    capacity = slot_tokens.shape[2]
    bit_index = lax.axis_size("expert").bit_length() - 2
    position = lax.axis_index("expert")
    half_count = swap_pairs.shape[0]
    own_swap = (
        jnp.sum(jnp.where(jnp.arange(half_count) == position % half_count, swap_pairs, 0)) > 0
    )
    live_slots = (
        (jnp.arange(capacity)[None, :] < slot_counts[0][:, None]).astype(jnp.float32).reshape(-1)
    )
    weighted = live_slots * slot_gates[0].reshape(-1)
    slot_route = slot_tokens[0].reshape(-1)
    matcher = (jnp.arange(tok_count)[:, None] == slot_route[None, :]).astype(jnp.float32)
    gate_up = jnp.concatenate([gate_weight[0], up_weight[0]], axis=1)
    down_proj = down_weight[0]
    moment_one = first_moment[0]
    moment_two = second_moment[0]
    moved_gate_up, moved_down = partner((gate_up, down_proj), "expert", bit_index)
    gate_up = jnp.where(own_swap, moved_gate_up, gate_up)
    down_proj = jnp.where(own_swap, moved_down, down_proj)
    moved_one, moved_two = (
        partner(moment_one.astype(jnp.bfloat16), "expert", bit_index).astype(moment_one.dtype),
        partner(moment_two.astype(jnp.bfloat16), "expert", bit_index).astype(moment_two.dtype),
    )
    moment_one = jnp.where(own_swap, moved_one, moment_one)
    moment_two = jnp.where(own_swap, moved_two, moment_two)

    def to_hosts(slot_rows):
        return held_order(slot_rows, swap_pairs)

    picked = jnp.take(tokens, slot_route, axis=0)
    outgoing = jnp.where(live_slots[:, None] > 0, picked, jnp.zeros_like(picked)).reshape(
        experts, capacity, model_cols
    )
    arrived = lax.all_to_all(
        to_hosts(outgoing), "expert", split_axis=0, concat_axis=0, tiled=True
    ).reshape(-1, model_cols)
    hidden_units = down_proj.shape[0]
    contract_last = (((1,), (1,)), ((), ()))
    preact = lax.psum(
        jnp.dot(arrived, gate_up, preferred_element_type=jnp.float32).astype(jnp.bfloat16), "dp"
    ).astype(jnp.float32)
    gate_pre = preact[:, :hidden_units]
    up_pre = preact[:, hidden_units:]
    hidden = (jax.nn.silu(gate_pre) * up_pre).astype(jnp.bfloat16)
    outputs = (
        jnp.dot(hidden, down_proj, preferred_element_type=jnp.float32)
        .astype(jnp.bfloat16)
        .reshape(-1, capacity, model_cols)
    )
    returned = to_hosts(
        lax.all_to_all(outputs, "expert", split_axis=0, concat_axis=0, tiled=True)
    ).reshape(-1, model_cols)
    mixed = jnp.dot(
        matcher * weighted[None, :], returned.astype(jnp.float32), precision=lax.Precision.HIGHEST
    ).astype(jnp.bfloat16)
    grad_picked = jnp.take(cotangent, slot_route, axis=0).astype(jnp.float32) * weighted[:, None]
    grad_slots = grad_picked.astype(jnp.bfloat16).reshape(experts, capacity, model_cols)
    arrived_grad = lax.all_to_all(
        to_hosts(grad_slots), "expert", split_axis=0, concat_axis=0, tiled=True
    ).reshape(-1, model_cols)
    weight_grad = lax.dot_general(
        hidden, arrived_grad, (((0,), (0,)), ((), ())), preferred_element_type=jnp.float32
    )
    hidden_grad = lax.psum(
        lax.dot_general(
            arrived_grad, down_proj, contract_last, preferred_element_type=jnp.float32
        ).astype(jnp.bfloat16),
        "dp",
    ).astype(jnp.float32)
    back_rows = lax.dot_general(
        preact_grad(hidden_grad, gate_pre, up_pre),
        gate_up,
        contract_last,
        preferred_element_type=jnp.float32,
    ).astype(jnp.bfloat16)
    returned_grad = to_hosts(
        lax.all_to_all(
            back_rows.reshape(-1, capacity, model_cols),
            "expert",
            split_axis=0,
            concat_axis=0,
            tiled=True,
        )
    ).reshape(-1, model_cols)
    token_grad = jnp.dot(
        matcher * live_slots[None, :],
        returned_grad.astype(jnp.float32),
        precision=lax.Precision.HIGHEST,
    ).astype(jnp.bfloat16)
    new_one = beta_first * moment_one + (1.0 - beta_first) * weight_grad
    new_two = beta_second * moment_two + (1.0 - beta_second) * weight_grad * weight_grad
    step_dir = (new_one / (jnp.sqrt(new_two) + adam_eps)).astype(jnp.bfloat16)
    return (mixed, token_grad, new_one[None], new_two[None], step_dir[None])


def solution(mesh):
    return jax.shard_map(
        shards,
        mesh=mesh,
        in_specs=(
            P("expert", "dp"),
            P("expert", "dp"),
            P("expert", None, None),
            P("expert", None),
            P("expert", None, None),
            P(),
            P("expert", "dp", None),
            P("expert", "dp", None),
            P("expert", None, "dp"),
            P("expert", None, "dp"),
            P("expert", None, "dp"),
        ),
        out_specs=(
            P("expert", "dp"),
            P("expert", "dp"),
            P("expert", None, "dp"),
            P("expert", None, "dp"),
            P("expert", None, "dp"),
        ),
        check_vma=False,
    )
```

profile of v0, /device:TPU:1, one launch (start us, length us, event | category | flops | bytes accessed | tf_op | source)
XLA Modules:
  0.0 329.5 jit_solution(159144839303572518)
XLA Ops:
  7.2 0.8 eq.24
  8.0 0.7 iota_compare_fusion.3
  8.7 0.1 lt.50
  8.8 1.1 copy.22
  9.9 1.1 copy.24
  11.0 4.0 %gather_fusion = bf16[1024,448]{1,0:T(8,128)(2,1)S(1)} fusion(bf16[256,448]{1,0:T(8,128)(2,1)S(1)} %copy.22, s32[1024]{0:T(1024)S(1)} %fusion.26), kind=kCustom, calls=%fused_computation.clone | custom fusion | bytes 1839104 | tf_op jit(solution)/shard_map/jit(_take)/gather | solution.py:80
  14.9 0.0 copy-start.6
  14.9 0.0 copy-start.8
  15.0 4.0 %gather_fusion.1 = bf16[1024,448]{1,0:T(8,128)(2,1)S(1)} fusion(bf16[256,448]{1,0:T(8,128)(2,1)S(1)} %copy.24, s32[1024]{0:T(1024)S(1)} %fusion.26), kind=kCustom, calls=%fused_computation.1.clone | custom fusion | bytes 1839104 | tf_op jit(solution)/shard_map/jit(_take)/gather | solution.py:106
  18.9 0.0 copy-done.6
  18.9 0.1 reshape_squeeze.4
  19.0 0.0 copy-done.8
  19.0 0.8 select_select_fusion
  19.8 0.3 multiply_convert_fusion.1
  20.2 2.2 reverse_select_fusion.1
  22.4 11.9 %all-to-all-start.2 = ((bf16[32,32,448]{2,1,0:T(8,128)(2,1)}), bf16[32,32,448]{2,1,0:T(8,128)(2,1)S(1)}, u32[]{:S(2)}, u32[]{:S(2)}) async-start(bf16[32,32,448]{2,1,0:T(8,128)(2,1)} %bitcast.11), calls=%async_computation.2 | async-start | bytes 2097152 | tf_op jit(solution)/shard_map/all_to_all | solution.py:108
  34.2 1.6 pad_maximum_fusion
  35.8 2.8 collective-permute-start
  38.6 20.5 %all-to-all-done.2 = bf16[32,32,448]{2,1,0:T(8,128)(2,1)S(1)} async-done(((bf16[32,32,448]{2,1,0:T(8,128)(2,1)}), bf16[32,32,448]{2,1,0:T(8,128)(2,1)S(1)}, u32[]{:S(2)}, u32[]{:S(2)}) %all-to-all-start.2) | async-done | bytes 917536 | tf_op jit(solution)/shard_map/all_to_all | solution.py:108
  59.1 0.0 copy-start.4
  59.1 8.4 %all-to-all-start = ((bf16[32,32,448]{2,1,0:T(8,128)(2,1)}), bf16[32,32,448]{2,1,0:T(8,128)(2,1)}, u32[]{:S(2)}, u32[]{:S(2)}) async-start(bf16[32,32,448]{2,1,0:T(8,128)(2,1)} %bitcast.2), calls=%async_computation | async-start | bytes 2097152 | tf_op jit(solution)/shard_map/all_to_all | solution.py:84
  67.6 0.0 all-reduce.3.cloned.1.call-start
  67.6 2.8 collective-permute-start.1
  70.4 0.6 fusion.27
  71.6 48.7 %collective-permute-done.1 = bf16[1024,448]{0,1:T(8,128)(2,1)} collective-permute-done((bf16[1024,448]{0,1:T(8,128)(2,1)}, bf16[1024,448]{0,1:T(8,128)(2,1)}, u32[]{:S(2)}, u32[]{:S(2)}) %collective-permute-start.1) | collective-permute-done | bytes 917536 | tf_op jit(solution)/shard_map/ppermute | solution.py:18
  120.3 3.8 %convolution_convert_fusion.1 = bf16[1024,1024]{1,0:T(8,128)(2,1)} fusion(bf16[1024,448]{1,0:T(8,128)(2,1)S(1)} %bitcast.65, bf16[1024,448]{0,1:T(8,128)(2,1)} %collective-permute-done.1, pred[]{:T(512)S(6)} %gt.21, bf16[1,1024,448]{1,2,0:T(8,128)(2,1)} %param.21), kind=kOutput, calls=%fused_computation.18 | convolution fusion | flops 941031424 | bytes 4849665 | tf_op jit(solution)/shard_map/dot_general | solution.py:115
  124.2 0.0 copy-done.4
  124.2 0.0 all-to-all-done
  124.2 0.0 collective-permute-done
  124.2 6.1 %convolution_convert_fusion = bf16[1024,2048]{1,0:T(8,128)(2,1)} fusion(bf16[1024,448]{1,0:T(8,128)(2,1)} %bitcast.3, bf16[448,2048]{1,0:T(8,128)(2,1)} %collective-permute-done, pred[]{:T(512)S(6)} %gt.21, bf16[448,1024]{1,0:T(8,128)(2,1)} %bitcast.68, bf16[448,1024]{1,0:T(8,128)(2,1)} %bitcast.71), kind=kOutput, calls=%fused_computation.15 | convolution fusion | flops 1885732864 | bytes 8781825 | tf_op jit(solution)/shard_map/dot_general | solution.py:90
  130.3 0.0 all-reduce.3.cloned.1.call-update
  130.3 90.2 %all-reduce.3.cloned.1.call-done = (bf16[1024,2048]{1,0:T(8,128)(2,1)}, bf16[1024,1024]{1,0:T(8,128)(2,1)}) async-done(((bf16[1024,2048]{1,0:T(8,128)(2,1)}, bf16[1024,1024]{1,0:T(8,128)(2,1)}), (bf16[1024,2048]{1,0:T(8,128)(2,1)}, bf16[1024,1024]{1,0:T(8,128)(2,1)})) %all-reduce.3.cloned.1.call-update) | async-done | bytes 6291472 | tf_op jit(solution)/shard_map/psum | solution.py:89
  220.5 0.0 copy-start.3
  220.5 3.4 %convert_element_type.69 = f32[1024,2048]{1,0:T(8,128)S(1)} convert(bf16[1024,2048]{1,0:T(8,128)(2,1)} %get-tuple-element.6) | non-fusion elementwise | flops 2097152 | bytes 12582912 | tf_op jit(solution)/shard_map/convert_element_type | solution.py:91
  223.9 0.0 copy-done.3
  223.9 0.0 copy-start.7
  224.0 3.7 %fusion.2 = (bf16[1024,1024]{1,0:T(8,128)(2,1)S(1)}, bf16[1024,1024]{1,0:T(8,128)(2,1)}, bf16[1024,1024]{1,0:T(8,128)(2,1)S(1)}) fusion(bf16[1024,1024]{1,0:T(8,128)(2,1)S(1)} %copy-done.3, f32[1024,2048]{1,0:T(8,128)S(1)} %convert_element_type.69), kind=kLoop, calls=%fused_computation.6 | loop fusion | flops 17825792 | bytes 16777216 | tf_op jit(solution)/shard_map/convert
  227.6 0.0 copy-start
  227.6 1.3 copy-done
  229.0 0.0 copy-done.7
  229.0 1.1 convolution_convert_fusion.2
  230.1 1.3 copy.23
  231.4 10.7 %all-to-all-start.1 = ((bf16[32,32,448]{2,1,0:T(8,128)(2,1)}), bf16[32,32,448]{2,1,0:T(8,128)(2,1)S(1)}, u32[]{:S(2)}, u32[]{:S(2)}) async-start(bf16[32,32,448]{2,1,0:T(8,128)(2,1)} %bitcast.7), calls=%async_computation.1 | async-start | bytes 2097152 | tf_op jit(solution)/shard_map/all_to_all | solution.py:101
  242.2 0.0 copy-start.2
  242.2 2.7 bitcast_convert_fusion.1
  244.9 2.7 collective-permute-start.2
  247.6 0.0 copy-done.2
  247.6 4.6 %fusion.13 = bf16[1024,448]{0,1:T(8,128)(2,1)} fusion(bf16[1024,1024]{1,0:T(8,128)(2,1)S(1)} %copy-done.2, bf16[1024,1024]{1,0:T(8,128)(2,1)S(1)} %get-tuple-element.8, bf16[448,2048]{1,0:T(8,128)(2,1)} %collective-permute-done, pred[]{:T(512)S(6)} %gt.21, bf16[448,1024]{1,0:T(8,128)(2,1)} %bitcast.69, bf16[448,1024]{1,0:T(8,128)(2,1)} %bitcast.72), kind=kOutput, calls=%fused_computation.34 | convolution fusion | flops 1892483072 | bytes 8781825 | tf_op jit(solution)/shard_map/dot_general | solution.py:120
  252.3 2.2 copy.25
  254.5 12.8 %all-to-all-done.1 = bf16[32,32,448]{2,1,0:T(8,128)(2,1)S(1)} async-done(((bf16[32,32,448]{2,1,0:T(8,128)(2,1)}), bf16[32,32,448]{2,1,0:T(8,128)(2,1)S(1)}, u32[]{:S(2)}, u32[]{:S(2)}) %all-to-all-start.1) | async-done | bytes 917536 | tf_op jit(solution)/shard_map/all_to_all | solution.py:101
  267.3 0.0 copy-start.5
  267.3 8.2 %all-to-all-start.3 = ((bf16[32,32,448]{2,1,0:T(8,128)(2,1)}), bf16[32,32,448]{2,1,0:T(8,128)(2,1)S(1)}, u32[]{:S(2)}, u32[]{:S(2)}) async-start(bf16[32,32,448]{2,1,0:T(8,128)(2,1)} %bitcast.13), calls=%async_computation.3 | async-start | bytes 2097152 | tf_op jit(solution)/shard_map/all_to_all | solution.py:127
  275.5 0.0 copy-start.1
  275.5 1.8 bitcast_convert_fusion
  277.3 2.8 collective-permute-start.3
  280.1 0.0 collective-permute-done.2
  280.1 30.9 %collective-permute-done.3 = bf16[1024,448]{0,1:T(8,128)(2,1)S(1)} collective-permute-done((bf16[1024,448]{0,1:T(8,128)(2,1)S(1)}, bf16[1024,448]{0,1:T(8,128)(2,1)S(1)}, u32[]{:S(2)}, u32[]{:S(2)}) %collective-permute-start.3) | collective-permute-done | bytes 917536 | tf_op jit(solution)/shard_map/ppermute | solution.py:18
  311.0 0.0 copy-done.5
  311.0 0.0 copy-done.1
  311.0 6.7 %fusion.18 = (bf16[1,1024,448]{1,2,0:T(8,128)(2,1)}, f32[1,1024,448]{1,2,0:T(8,128)}, f32[1,1024,448]{1,2,0:T(8,128)}) fusion(f32[1,1024,448]{1,2,0:T(8,128)} %param.22, bf16[1024,448]{0,1:T(8,128)(2,1)} %collective-permute-done.2, pred[]{:T(512)S(6)} %gt.21, f32[1,1024,448]{1,2,0:T(8,128)} %param.23, bf16[1024,448]{0,1:T(8,128)(2,1)S(1)} %collective-permute-done.3, ...), kind=kOutput, calls=%fused_computation.42 | convolution fusion | flops 945946624 | bytes 13107201 | tf_op jit(solution)/shard_map/dot_general | solution.py:111
  317.7 0.0 all-to-all-done.3
  317.7 0.9 reverse_select_fusion
  318.6 2.0 convolution_convert_fusion.4
  320.6 2.0 convolution_convert_fusion.3
  (4 shorter events, 0.0 us)
Async XLA Ops:
  14.9 4.0 %copy-start.6 = (f32[1,32,32]{2,1,0:T(8,128)S(1)}, f32[1,32,32]{2,1,0:T(8,128)}, u32[]{:S(2)}) copy-start(f32[1,32,32]{2,1,0:T(8,128)} %param.17) | copy-start | bytes 12292
  14.9 4.1 %copy-start.8 = (s32[16]{0:T(128)S(1)}, s32[16]{0:T(128)}, u32[]{:S(2)}) copy-start(s32[16]{0:T(128)} %param.18) | copy-start | bytes 196
  22.4 36.8 %all-to-all-start.2 = ((bf16[32,32,448]{2,1,0:T(8,128)(2,1)}), bf16[32,32,448]{2,1,0:T(8,128)(2,1)S(1)}, u32[]{:S(2)}, u32[]{:S(2)}) async-start(bf16[32,32,448]{2,1,0:T(8,128)(2,1)} %bitcast.11), calls=%async_computation.2 | async-start | bytes 2097152 | tf_op jit(solution)/shard_map/all_to_all | solution.py:108
  35.8 88.4 %collective-permute-start = (bf16[448,2048]{1,0:T(8,128)(2,1)S(1)}, bf16[448,2048]{1,0:T(8,128)(2,1)}, u32[]{:S(2)}, u32[]{:S(2)}) collective-permute-start(bf16[448,2048]{1,0:T(8,128)(2,1)S(1)} %pad_maximum_fusion), channel_id=1, source_target_pairs={{0,16},{16,0},{1,17},{17,1},{2,18},{18,2},{3,19},{19,3},{4,20},{20... | collective-permute-start | bytes 5505032 | tf_op jit(solution)/shard_map/ppermute | solution.py:18
  59.1 65.1 %copy-start.4 = (bf16[32,32,448]{2,1,0:T(8,128)(2,1)}, bf16[32,32,448]{2,1,0:T(8,128)(2,1)S(1)}, u32[]{:S(2)}) copy-start(bf16[32,32,448]{2,1,0:T(8,128)(2,1)S(1)} %all-to-all-done.2) | copy-start | bytes 2752516
  59.1 65.1 %all-to-all-start = ((bf16[32,32,448]{2,1,0:T(8,128)(2,1)}), bf16[32,32,448]{2,1,0:T(8,128)(2,1)}, u32[]{:S(2)}, u32[]{:S(2)}) async-start(bf16[32,32,448]{2,1,0:T(8,128)(2,1)} %bitcast.2), calls=%async_computation | async-start | bytes 2097152 | tf_op jit(solution)/shard_map/all_to_all | solution.py:84
  67.6 153.0 %all-reduce.3.cloned.1.call-start = ((), (), s32[]{:S(2)}) async-start(), calls=%async_computation.4 | async-start | bytes 12582912 | tf_op jit(solution)/shard_map/psum | solution.py:89
  67.6 52.7 %collective-permute-start.1 = (bf16[1024,448]{0,1:T(8,128)(2,1)}, bf16[1024,448]{0,1:T(8,128)(2,1)}, u32[]{:S(2)}, u32[]{:S(2)}) collective-permute-start(bf16[1024,448]{0,1:T(8,128)(2,1)} %bitcast.74), channel_id=1, source_target_pairs={{0,16},{16,0},{1,17},{17,1},{2,18},{18,2},{3,19},{19,3},{4,20},{20... | collective-permute-start | bytes 2752520 | tf_op jit(solution)/shard_map/ppermute | solution.py:18
  220.5 3.4 %copy-start.3 = (bf16[1024,1024]{1,0:T(8,128)(2,1)S(1)}, bf16[1024,1024]{1,0:T(8,128)(2,1)}, u32[]{:S(2)}) copy-start(bf16[1024,1024]{1,0:T(8,128)(2,1)} %get-tuple-element.7) | copy-start | bytes 6291460
  223.9 5.0 %copy-start.7 = (bf16[1,1024,448]{1,2,0:T(8,128)(2,1)S(1)}, bf16[1,1024,448]{1,2,0:T(8,128)(2,1)}, u32[]{:S(2)}) copy-start(bf16[1,1024,448]{1,2,0:T(8,128)(2,1)} %param.21) | copy-start | bytes 2752516
  227.6 1.3 copy-start
  231.4 35.9 %all-to-all-start.1 = ((bf16[32,32,448]{2,1,0:T(8,128)(2,1)}), bf16[32,32,448]{2,1,0:T(8,128)(2,1)S(1)}, u32[]{:S(2)}, u32[]{:S(2)}) async-start(bf16[32,32,448]{2,1,0:T(8,128)(2,1)} %bitcast.7), calls=%async_computation.1 | async-start | bytes 2097152 | tf_op jit(solution)/shard_map/all_to_all | solution.py:101
  242.2 5.5 %copy-start.2 = (bf16[1024,1024]{1,0:T(8,128)(2,1)S(1)}, bf16[1024,1024]{1,0:T(8,128)(2,1)}, u32[]{:S(2)}) copy-start(bf16[1024,1024]{1,0:T(8,128)(2,1)} %get-tuple-element.9) | copy-start | bytes 6291460
  244.9 35.3 %collective-permute-start.2 = (bf16[1024,448]{0,1:T(8,128)(2,1)}, bf16[1024,448]{0,1:T(8,128)(2,1)}, u32[]{:S(2)}, u32[]{:S(2)}) collective-permute-start(bf16[1024,448]{0,1:T(8,128)(2,1)} %bitcast_convert_fusion.1), channel_id=1, source_target_pairs={{0,16},{16,0},{1,17},{17,1},{2,18},{18,2},{3,19},{19,3},{4,20},{20... | collective-permute-start | bytes 2752520 | tf_op jit(solution)/shard_map/ppermute | solution.py:18
  267.3 43.7 %copy-start.5 = (bf16[32,32,448]{2,1,0:T(8,128)(2,1)S(1)}, bf16[32,32,448]{2,1,0:T(8,128)(2,1)}, u32[]{:S(2)}) copy-start(bf16[32,32,448]{2,1,0:T(8,128)(2,1)} %copy-done.4) | copy-start | bytes 2752516
  267.3 50.4 %all-to-all-start.3 = ((bf16[32,32,448]{2,1,0:T(8,128)(2,1)}), bf16[32,32,448]{2,1,0:T(8,128)(2,1)S(1)}, u32[]{:S(2)}, u32[]{:S(2)}) async-start(bf16[32,32,448]{2,1,0:T(8,128)(2,1)} %bitcast.13), calls=%async_computation.3 | async-start | bytes 2097152 | tf_op jit(solution)/shard_map/all_to_all | solution.py:127
  275.5 35.5 %copy-start.1 = (bf16[1024,1024]{1,0:T(8,128)(2,1)S(1)}, bf16[1024,1024]{1,0:T(8,128)(2,1)}, u32[]{:S(2)}) copy-start(bf16[1024,1024]{1,0:T(8,128)(2,1)} %copy-done) | copy-start | bytes 6291460
  277.3 33.7 %collective-permute-start.3 = (bf16[1024,448]{0,1:T(8,128)(2,1)S(1)}, bf16[1024,448]{0,1:T(8,128)(2,1)S(1)}, u32[]{:S(2)}, u32[]{:S(2)}) collective-permute-start(bf16[1024,448]{0,1:T(8,128)(2,1)S(1)} %bitcast_convert_fusion), channel_id=1, source_target_pairs={{0,16},{16,0},{1,17},{17,1},{2,18},{18,2},{3,19},{19,3},{4,20},{20... | collective-permute-start | bytes 2752520 | tf_op jit(solution)/shard_map/ppermute | solution.py:18
Sparse Core Ops, SparseCore 0:
  130.4 90.0 all-reduce.2
where the time goes:
time: 330 us
  waiting for transfers between devices  203 us (62%)
  starting transfers between devices  50.4 us (15%)
  matrix products  26.5 us (8%)
  other arithmetic  18.7 us (6%)
  local copies, waits for them, and re-layouts  15.9 us (5%)
  between operations  14.9 us (5%)
    psum x1, waiting for transfers between devices, shards(): lax.psum(jnp.dot(arrived, gate_up, preferred_element_type=jnp.float32).as...  90.2 us
    ppermute x4, waiting for transfers between devices, partner(): return lax.ppermute(block, axis, route)  79.5 us
    all_to_all x1, waiting for transfers between devices, shards(): lax.all_to_all(to_hosts(grad_slots), 'expert', split_axis=0, concat_axis=...  20.5 us
    all_to_all x1, waiting for transfers between devices, shards(): lax.all_to_all(outputs, 'expert', split_axis=0, concat_axis=0, tiled=True)  12.8 us
    all_to_all x1, starting transfers between devices, shards(): lax.all_to_all(to_hosts(grad_slots), 'expert', split_axis=0, concat_axis=...  11.9 us
    ppermute x4, starting transfers between devices, partner(): return lax.ppermute(block, axis, route)  11.2 us
    all_to_all x1, starting transfers between devices, shards(): lax.all_to_all(outputs, 'expert', split_axis=0, concat_axis=0, tiled=True)  10.7 us
    all_to_all x1, starting transfers between devices, shards(): lax.all_to_all(to_hosts(outgoing), 'expert', split_axis=0, concat_axis=0,...  8.45 us
  transfers between devices with their start and end apart: 9, of which 5 were waited for; matrix products, arithmetic and copies ran while one was open for 7% of the time, Pallas kernels for 0%

commit v1 on v0

--- a/solution.py
+++ b/solution.py
@@ -86,7 +86,12 @@
     ).reshape(-1, model_cols)
     hidden_units = down_proj.shape[0]
     contract_last = (((1,), (1,)), ((), ()))
-    preact = lax.psum(
+
+    def units_connect(buf, chip_axis):
+        a_now = lax.all_gather(buf, chip_axis)
+        return jnp.sum(a_now, 0)
+
+    preact = units_connect(
         jnp.dot(arrived, gate_up, preferred_element_type=jnp.float32).astype(jnp.bfloat16), "dp"
     ).astype(jnp.float32)
     gate_pre = preact[:, :hidden_units]

time: 330 us -> 415 us (1.26); the launches traced: 330 us -> 407 us
  waiting for transfers between devices: 203 us -> 263 us
  other arithmetic: 18.7 us -> 39.6 us
    all_gather x0 -> x1, waiting for transfers between devices: none -> 116 us  [units_connect(): a_now = lax.all_gather(buf, chip_axis)]
    psum x1, waiting for transfers between devices: 90.2 us -> 51.2 us  [shards(): lax.psum(lax.dot_general(arrived_grad, down_proj, contract_last, preferre...]
    all_to_all x1, waiting for transfers between devices: 0.01 us -> 28.9 us  [shards(): lax.all_to_all(to_hosts(outgoing), 'expert', split_axis=0, concat_axis=0,...]
    ppermute x4, waiting for transfers between devices: 79.5 us -> 56 us  [partner(): return lax.ppermute(block, axis, route)]
    all_to_all x1, waiting for transfers between devices: 20.5 us -> 0.01 us  [shards(): lax.all_to_all(to_hosts(grad_slots), 'expert', split_axis=0, concat_axis=...]
    reduce_sum x0 -> x1, other arithmetic: none -> 14.3 us  [units_connect(): return jnp.sum(a_now, 0)]
  transfers between devices with their start and end apart: 9 -> 10, of which waited for: 5 -> 6; matrix products, arithmetic and copies ran while one was open for 7% -> 13% of each run, Pallas kernels for 0% -> 0%
where the time goes in v1:
time: 415 us; the launch traced here: 407 us
  waiting for transfers between devices  263 us (63%)
  starting transfers between devices  51.7 us (12%)
  other arithmetic  39.6 us (10%)
  matrix products  23.6 us (6%)
  between operations  14.9 us (4%)
  local copies, waits for them, and re-layouts  13.4 us (3%)
    all_gather x1, waiting for transfers between devices, units_connect(): a_now = lax.all_gather(buf, chip_axis)  116 us
    ppermute x4, waiting for transfers between devices, partner(): return lax.ppermute(block, axis, route)  56 us
    psum x1, waiting for transfers between devices, shards(): lax.psum(lax.dot_general(arrived_grad, down_proj, contract_last, preferre...  51.2 us
    all_to_all x1, waiting for transfers between devices, shards(): lax.all_to_all(to_hosts(outgoing), 'expert', split_axis=0, concat_axis=0,...  28.9 us
    reduce_sum x1, other arithmetic, units_connect(): return jnp.sum(a_now, 0)  14.3 us
    all_to_all x1, starting transfers between devices, shards(): lax.all_to_all(to_hosts(grad_slots), 'expert', split_axis=0, concat_axis=...  12.7 us
    ppermute x4, starting transfers between devices, partner(): return lax.ppermute(block, axis, route)  12.4 us
    all_to_all x1, waiting for transfers between devices, shards(): lax.all_to_all(outputs, 'expert', split_axis=0, concat_axis=0, tiled=True)  11.2 us
  transfers between devices with their start and end apart: 10, of which 6 were waited for; matrix products, arithmetic and copies ran while one was open for 13% of the time, Pallas kernels for 0%

profile of v1, /device:TPU:1, one launch (start us, length us, event | category | flops | bytes accessed | tf_op | source)
XLA Modules:
  0.0 406.6 jit_solution(8459296728860079441)
XLA Ops:
  7.2 0.0 copy-start.9
  7.2 0.0 copy-start.11
  7.2 0.0 copy-start.7
  7.2 0.0 copy-start.8
  7.2 2.9 pad_maximum_fusion
  10.1 3.6 collective-permute-start
  13.7 0.1 eq.24
  13.8 0.0 copy-done.11
  13.8 0.1 iota_compare_fusion.3
  13.8 0.1 lt.50
  14.0 0.1 copy.22
  14.1 0.0 copy-done.8
  14.1 0.1 copy.24
  14.3 4.0 gather_fusion
  18.2 0.0 copy-start.10
  18.3 0.0 copy-start.16
  18.3 4.0 gather_fusion.1
  22.2 0.1 reshape_squeeze.4
  22.3 0.0 copy-done.16
  22.3 0.8 select_select_fusion
  23.1 0.3 multiply_convert_fusion.1
  23.5 2.2 reverse_select_fusion.1
  25.7 9.3 %all-to-all-start = ((bf16[32,32,448]{2,1,0:T(8,128)(2,1)}), bf16[32,32,448]{2,1,0:T(8,128)(2,1)S(1)}, u32[]{:S(2)}, u32[]{:S(2)}) async-start(bf16[32,32,448]{2,1,0:T(8,128)(2,1)} %bitcast.2), calls=%async_computation | async-start | bytes 2097152 | tf_op jit(solution)/shard_map/all_to_all | solution.py:84
  35.0 0.0 all-gather.3.cloned.1.call-start
  35.0 0.6 fusion.27
  36.3 28.9 %all-to-all-done = bf16[32,32,448]{2,1,0:T(8,128)(2,1)S(1)} async-done(((bf16[32,32,448]{2,1,0:T(8,128)(2,1)}), bf16[32,32,448]{2,1,0:T(8,128)(2,1)S(1)}, u32[]{:S(2)}, u32[]{:S(2)}) %all-to-all-start) | async-done | bytes 917536 | tf_op jit(solution)/shard_map/all_to_all | solution.py:84
  65.3 0.0 collective-permute-done
  65.3 0.0 copy-done.6
  65.3 4.5 %convolution_convert_fusion = bf16[1024,2048]{1,0:T(8,128)(2,1)} fusion(bf16[1024,448]{1,0:T(8,128)(2,1)S(1)} %bitcast.69, bf16[448,2048]{1,0:T(8,128)(2,1)} %collective-permute-done, pred[]{:T(512)S(6)} %gt.21, bf16[448,1024]{1,0:T(8,128)(2,1)S(1)} %bitcast.72, bf16[448,1024]{1,0:T(8,128)(2,1)S(1)} %bitcast.75), kind=kOutput, calls=%fused_computation.15 | convolution fusion | flops 1885732864 | bytes 8781825 | tf_op jit(solution)/shard_map/dot_general | solution.py:95
  69.7 0.0 all-gather.3.cloned.1.call-update
  69.7 0.0 copy-start.12
  69.8 12.7 %all-to-all-start.2 = ((bf16[32,32,448]{2,1,0:T(8,128)(2,1)}), bf16[32,32,448]{2,1,0:T(8,128)(2,1)S(1)}, u32[]{:S(2)}, u32[]{:S(2)}) async-start(bf16[32,32,448]{2,1,0:T(8,128)(2,1)} %bitcast.12), calls=%async_computation.2 | async-start | bytes 2097152 | tf_op jit(solution)/shard_map/all_to_all | solution.py:113
  82.4 0.0 all-reduce.2.cloned.1.call-start
  82.5 3.0 collective-permute-start.1
  85.5 29.8 %collective-permute-done.1 = bf16[1024,448]{0,1:T(8,128)(2,1)S(1)} collective-permute-done((bf16[1024,448]{0,1:T(8,128)(2,1)S(1)}, bf16[1024,448]{0,1:T(8,128)(2,1)S(1)}, u32[]{:S(2)}, u32[]{:S(2)}) %collective-permute-start.1) | collective-permute-done | bytes 917536 | tf_op jit(solution)/shard_map/ppermute | solution.py:18
  115.3 0.0 all-to-all-done.2
  115.3 2.6 convolution_convert_fusion.1
  118.0 0.0 all-reduce.2.cloned.1.call-update
  118.0 116.0 %all-gather.3.cloned.1.call-done = bf16[8192,2048]{1,0:T(8,128)(2,1)} async-done(((bf16[1024,2048]{1,0:T(8,128)(2,1)}), bf16[8192,2048]{1,0:T(8,128)(2,1)}) %all-gather.3.cloned.1.call-update) | async-done | bytes 33554448 | tf_op jit(solution)/shard_map/all_gather | solution.py:91
  234.0 14.3 %reduce_sum.22 = bf16[1024,2048]{1,0:T(8,128)(2,1)} reduce(bf16[8,1024,2048]{2,1,0:T(8,128)(2,1)} %bitcast.60, bf16[]{:T(256)} %constant.22.clone.1), dimensions={0}, to_apply=%region_1.3 | reduce | flops 14680064 | bytes 37748736 | tf_op jit(solution)/shard_map/reduce_sum | solution.py:92
  248.2 6.5 %convert_element_type.71 = f32[1024,2048]{1,0:T(8,128)} convert(bf16[1024,2048]{1,0:T(8,128)(2,1)} %reduce_sum.22) | non-fusion elementwise | flops 2097152 | bytes 12582912 | tf_op jit(solution)/shard_map/convert_element_type | solution.py:96
  254.8 51.2 %all-reduce.2.cloned.1.call-done = bf16[1024,1024]{1,0:T(8,128)(2,1)} async-done(((bf16[1024,1024]{1,0:T(8,128)(2,1)}), bf16[1024,1024]{1,0:T(8,128)(2,1)}) %all-reduce.2.cloned.1.call-update) | async-done | bytes 2097168 | tf_op jit(solution)/shard_map/psum | solution.py:119
  306.0 6.5 %fusion.2 = (bf16[1024,1024]{1,0:T(8,128)(2,1)S(1)}, bf16[1024,1024]{1,0:T(8,128)(2,1)}, bf16[1024,1024]{1,0:T(8,128)(2,1)S(1)}) fusion(bf16[1024,1024]{1,0:T(8,128)(2,1)} %all-reduce.2.cloned.1.call-done, f32[1024,2048]{1,0:T(8,128)} %convert_element_type.71), kind=kLoop, calls=%fused_computation.6 | loop fusion | flops 17825792 | bytes 16777216 | tf_op jit(solution)/shard_map/convert.1
  312.4 1.3 copy-done
  313.8 0.0 copy-done.15
  313.8 1.2 convolution_convert_fusion.2
  315.0 1.3 copy.23
  316.3 9.5 %all-to-all-start.1 = ((bf16[32,32,448]{2,1,0:T(8,128)(2,1)}), bf16[32,32,448]{2,1,0:T(8,128)(2,1)S(1)}, u32[]{:S(2)}, u32[]{:S(2)}) async-start(bf16[32,32,448]{2,1,0:T(8,128)(2,1)} %bitcast.8), calls=%async_computation.1 | async-start | bytes 2097152 | tf_op jit(solution)/shard_map/all_to_all | solution.py:106
  325.8 2.7 bitcast_convert_fusion.1
  328.5 2.7 collective-permute-start.2
  331.3 0.0 copy-done.2
  331.3 4.6 %fusion.13 = bf16[1024,448]{0,1:T(8,128)(2,1)} fusion(bf16[1024,1024]{1,0:T(8,128)(2,1)S(1)} %copy-done.2, bf16[1024,1024]{1,0:T(8,128)(2,1)S(1)} %get-tuple-element.6, bf16[448,2048]{1,0:T(8,128)(2,1)} %collective-permute-done, pred[]{:T(512)S(6)} %gt.21, bf16[448,1024]{1,0:T(8,128)(2,1)} %bitcast.71, bf16[448,1024]{1,0:T(8,128)(2,1)} %bitcast.74), kind=kOutput, calls=%fused_computation.34 | convolution fusion | flops 1892483072 | bytes 8781825 | tf_op jit(solution)/shard_map/dot_general | solution.py:125
  335.9 2.2 copy.25
  338.1 11.2 %all-to-all-done.1 = bf16[32,32,448]{2,1,0:T(8,128)(2,1)S(1)} async-done(((bf16[32,32,448]{2,1,0:T(8,128)(2,1)}), bf16[32,32,448]{2,1,0:T(8,128)(2,1)S(1)}, u32[]{:S(2)}, u32[]{:S(2)}) %all-to-all-start.1) | async-done | bytes 917536 | tf_op jit(solution)/shard_map/all_to_all | solution.py:106
  349.3 7.8 %all-to-all-start.3 = ((bf16[32,32,448]{2,1,0:T(8,128)(2,1)}), bf16[32,32,448]{2,1,0:T(8,128)(2,1)S(1)}, u32[]{:S(2)}, u32[]{:S(2)}) async-start(bf16[32,32,448]{2,1,0:T(8,128)(2,1)} %bitcast.14), calls=%async_computation.3 | async-start | bytes 2097152 | tf_op jit(solution)/shard_map/all_to_all | solution.py:132
  357.1 1.8 bitcast_convert_fusion
  358.9 3.0 collective-permute-start.3
  361.9 0.0 collective-permute-done.2
  361.9 26.2 %collective-permute-done.3 = bf16[1024,448]{0,1:T(8,128)(2,1)S(1)} collective-permute-done((bf16[1024,448]{0,1:T(8,128)(2,1)S(1)}, bf16[1024,448]{0,1:T(8,128)(2,1)S(1)}, u32[]{:S(2)}, u32[]{:S(2)}) %collective-permute-start.3) | collective-permute-done | bytes 917536 | tf_op jit(solution)/shard_map/ppermute | solution.py:18
  388.1 6.7 %fusion.18 = (bf16[1,1024,448]{1,2,0:T(8,128)(2,1)}, f32[1,1024,448]{1,2,0:T(8,128)}, f32[1,1024,448]{1,2,0:T(8,128)}) fusion(f32[1,1024,448]{1,2,0:T(8,128)} %param.22, bf16[1024,448]{0,1:T(8,128)(2,1)} %collective-permute-done.2, pred[]{:T(512)S(6)} %gt.21, f32[1,1024,448]{1,2,0:T(8,128)} %param.23, bf16[1024,448]{0,1:T(8,128)(2,1)S(1)} %collective-permute-done.3, ...), kind=kOutput, calls=%fused_computation.42 | convolution fusion | flops 945946624 | bytes 13107201 | tf_op jit(solution)/shard_map/dot_general | solution.py:116
  394.8 0.0 all-to-all-done.3
  394.8 0.9 reverse_select_fusion
  395.7 2.0 convolution_convert_fusion.4
  397.7 2.0 convolution_convert_fusion.3
  (24 shorter events, 0.1 us)
Async XLA Ops:
  7.2 6.5 %copy-start.9 = (s32[1,32,32]{2,1,0:T(8,128)S(1)}, s32[1,32,32]{2,1,0:T(8,128)}, u32[]{:S(2)}) copy-start(s32[1,32,32]{2,1,0:T(8,128)} %param.15) | copy-start | bytes 12292
  7.2 6.6 %copy-start.11 = (s32[1,32]{1,0:T(1,128)S(1)}, s32[1,32]{1,0:T(1,128)}, u32[]{:S(2)}) copy-start(s32[1,32]{1,0:T(1,128)} %param.16) | copy-start | bytes 388
  7.2 6.8 %copy-start.7 = (bf16[256,448]{0,1:T(8,128)(2,1)S(1)}, bf16[256,448]{0,1:T(8,128)(2,1)}, u32[]{:S(2)}) copy-start(bf16[256,448]{0,1:T(8,128)(2,1)} %param.13) | copy-start | bytes 688132
  7.2 6.9 %copy-start.8 = (bf16[256,448]{0,1:T(8,128)(2,1)S(1)}, bf16[256,448]{0,1:T(8,128)(2,1)}, u32[]{:S(2)}) copy-start(bf16[256,448]{0,1:T(8,128)(2,1)} %param.14) | copy-start | bytes 688132
  10.1 55.1 %collective-permute-start = (bf16[448,2048]{1,0:T(8,128)(2,1)}, bf16[448,2048]{1,0:T(8,128)(2,1)}, u32[]{:S(2)}, u32[]{:S(2)}) collective-permute-start(bf16[448,2048]{1,0:T(8,128)(2,1)} %pad_maximum_fusion), channel_id=1, source_target_pairs={{0,16},{16,0},{1,17},{17,1},{2,18},{18,2},{3,19},{19,3},{4,20},{20... | collective-permute-start | bytes 5505032 | tf_op jit(solution)/shard_map/ppermute | solution.py:18
  18.2 4.0 copy-start.10
  18.3 4.1 %copy-start.16 = (s32[16]{0:T(128)S(1)}, s32[16]{0:T(128)}, u32[]{:S(2)}) copy-start(s32[16]{0:T(128)} %param.18) | copy-start | bytes 196
  25.7 39.6 %copy-start.5 = (bf16[1,448,1024]{2,1,0:T(8,128)(2,1)S(1)}, bf16[1,448,1024]{2,1,0:T(8,128)(2,1)}, u32[]{:S(2)}) copy-start(bf16[1,448,1024]{2,1,0:T(8,128)(2,1)} %param.20) | copy-start | bytes 2752516
  25.7 39.6 %copy-start.6 = (bf16[1,448,1024]{2,1,0:T(8,128)(2,1)S(1)}, bf16[1,448,1024]{2,1,0:T(8,128)(2,1)}, u32[]{:S(2)}) copy-start(bf16[1,448,1024]{2,1,0:T(8,128)(2,1)} %param.19) | copy-start | bytes 2752516
  25.7 39.6 %all-to-all-start = ((bf16[32,32,448]{2,1,0:T(8,128)(2,1)}), bf16[32,32,448]{2,1,0:T(8,128)(2,1)S(1)}, u32[]{:S(2)}, u32[]{:S(2)}) async-start(bf16[32,32,448]{2,1,0:T(8,128)(2,1)} %bitcast.2), calls=%async_computation | async-start | bytes 2097152 | tf_op jit(solution)/shard_map/all_to_all | solution.py:84
  35.0 199.0 %all-gather.3.cloned.1.call-start = ((), (), s32[]{:S(2)}) async-start(), calls=%async_computation.5 | async-start | bytes 37748736 | tf_op jit(solution)/shard_map/all_gather | solution.py:91
  69.7 12.7 %copy-start.12 = (bf16[1,1024,448]{1,2,0:T(8,128)(2,1)S(1)}, bf16[1,1024,448]{1,2,0:T(8,128)(2,1)}, u32[]{:S(2)}) copy-start(bf16[1,1024,448]{1,2,0:T(8,128)(2,1)} %param.21) | copy-start | bytes 2752516
  69.8 45.6 %all-to-all-start.2 = ((bf16[32,32,448]{2,1,0:T(8,128)(2,1)}), bf16[32,32,448]{2,1,0:T(8,128)(2,1)S(1)}, u32[]{:S(2)}, u32[]{:S(2)}) async-start(bf16[32,32,448]{2,1,0:T(8,128)(2,1)} %bitcast.12), calls=%async_computation.2 | async-start | bytes 2097152 | tf_op jit(solution)/shard_map/all_to_all | solution.py:113
  82.4 223.5 %all-reduce.2.cloned.1.call-start = ((), (), s32[]{:S(2)}) async-start(), calls=%async_computation.4 | async-start | bytes 4194304 | tf_op jit(solution)/shard_map/psum | solution.py:119
  82.5 32.8 %collective-permute-start.1 = (bf16[1024,448]{0,1:T(8,128)(2,1)S(1)}, bf16[1024,448]{0,1:T(8,128)(2,1)S(1)}, u32[]{:S(2)}, u32[]{:S(2)}) collective-permute-start(bf16[1024,448]{0,1:T(8,128)(2,1)S(1)} %bitcast.77), channel_id=1, source_target_pairs={{0,16},{16,0},{1,17},{17,1},{2,18},{18,2},{3,19},{19,3},{4,20},{20... | collective-permute-start | bytes 2752520 | tf_op jit(solution)/shard_map/ppermute | solution.py:18
  115.3 2.6 copy-start.14
  115.3 2.6 copy-start.3
  306.0 7.8 %copy-start.13 = (bf16[1,1024,448]{1,2,0:T(8,128)(2,1)S(1)}, bf16[1,1024,448]{1,2,0:T(8,128)(2,1)}, u32[]{:S(2)}) copy-start(bf16[1,1024,448]{1,2,0:T(8,128)(2,1)} %param.21) | copy-start | bytes 2752516
  306.0 7.8 %copy-start.15 = (bf16[1024,448]{0,1:T(8,128)(2,1)S(1)}, bf16[1024,448]{0,1:T(8,128)(2,1)}, u32[]{:S(2)}) copy-start(bf16[1024,448]{0,1:T(8,128)(2,1)} %copy-done.14) | copy-start | bytes 2752516
  312.4 1.3 copy-start
  316.3 33.1 %all-to-all-start.1 = ((bf16[32,32,448]{2,1,0:T(8,128)(2,1)}), bf16[32,32,448]{2,1,0:T(8,128)(2,1)S(1)}, u32[]{:S(2)}, u32[]{:S(2)}) async-start(bf16[32,32,448]{2,1,0:T(8,128)(2,1)} %bitcast.8), calls=%async_computation.1 | async-start | bytes 2097152 | tf_op jit(solution)/shard_map/all_to_all | solution.py:106
  325.8 5.5 %copy-start.2 = (bf16[1024,1024]{1,0:T(8,128)(2,1)S(1)}, bf16[1024,1024]{1,0:T(8,128)(2,1)}, u32[]{:S(2)}) copy-start(bf16[1024,1024]{1,0:T(8,128)(2,1)} %get-tuple-element.7) | copy-start | bytes 6291460
  328.5 33.4 %collective-permute-start.2 = (bf16[1024,448]{0,1:T(8,128)(2,1)}, bf16[1024,448]{0,1:T(8,128)(2,1)}, u32[]{:S(2)}, u32[]{:S(2)}) collective-permute-start(bf16[1024,448]{0,1:T(8,128)(2,1)} %bitcast_convert_fusion.1), channel_id=1, source_target_pairs={{0,16},{16,0},{1,17},{17,1},{2,18},{18,2},{3,19},{19,3},{4,20},{20... | collective-permute-start | bytes 2752520 | tf_op jit(solution)/shard_map/ppermute | solution.py:18
  349.3 38.8 %copy-start.4 = (bf16[32,32,448]{2,1,0:T(8,128)(2,1)S(1)}, bf16[32,32,448]{2,1,0:T(8,128)(2,1)}, u32[]{:S(2)}) copy-start(bf16[32,32,448]{2,1,0:T(8,128)(2,1)} %copy-done.3) | copy-start | bytes 2752516
  349.3 45.5 %all-to-all-start.3 = ((bf16[32,32,448]{2,1,0:T(8,128)(2,1)}), bf16[32,32,448]{2,1,0:T(8,128)(2,1)S(1)}, u32[]{:S(2)}, u32[]{:S(2)}) async-start(bf16[32,32,448]{2,1,0:T(8,128)(2,1)} %bitcast.14), calls=%async_computation.3 | async-start | bytes 2097152 | tf_op jit(solution)/shard_map/all_to_all | solution.py:132
  357.1 31.0 %copy-start.1 = (bf16[1024,1024]{1,0:T(8,128)(2,1)S(1)}, bf16[1024,1024]{1,0:T(8,128)(2,1)}, u32[]{:S(2)}) copy-start(bf16[1024,1024]{1,0:T(8,128)(2,1)} %copy-done) | copy-start | bytes 6291460
  358.9 29.2 %collective-permute-start.3 = (bf16[1024,448]{0,1:T(8,128)(2,1)S(1)}, bf16[1024,448]{0,1:T(8,128)(2,1)S(1)}, u32[]{:S(2)}, u32[]{:S(2)}) collective-permute-start(bf16[1024,448]{0,1:T(8,128)(2,1)S(1)} %bitcast_convert_fusion), channel_id=1, source_target_pairs={{0,16},{16,0},{1,17},{17,1},{2,18},{18,2},{3,19},{19,3},{4,20},{20... | collective-permute-start | bytes 2752520 | tf_op jit(solution)/shard_map/ppermute | solution.py:18
Sparse Core Ops, SparseCore 0:
  69.9 164.0 all-gather.2
  236.3 69.5 all-reduce.1
